TPU v7x, 32 devices: a whole 2x2x4 slice. The times are simulated.
32 devices in a mesh: inner: 8 (over z, y), cols: 4 (over x, core).
Axes of the slice: x: 2, y: 2, z: 4, core: 2. Of those that a mesh axis runs over, the one named last changes fastest.
Arguments:
- left_u: bfloat16 [64, 512, 128], P(('inner', 'cols')), may hold values from -6 to 6
- left_v: bfloat16 [64, 512, 128], P(('inner', 'cols')), may hold values from -0.0234375 to 0.0234375
- right_u: bfloat16 [16, 64, 512, 128], P('cols', 'inner'), may hold values from -6 to 6
- right_v: bfloat16 [16, 64, 512, 128], P('cols', 'inner'), may hold values from -0.1875 to 0.1875
- sketch: bfloat16 [16, 512, 128], P('cols'), may hold values from -0.25 to 0.25
- tile_index: int32 [16, 64], P('cols', 'inner'), may hold values from 0 to 63, as said below
- slot_mask: int32 [16, 64], P('cols', 'inner'), may hold values from 0 to 1, as said below
Outputs:
- basis: float32 [16, 512, 128], P('cols', 'inner')
- coeff: float32 [16, 512, 128], P('cols', 'inner')
Inputs may be any that keep to these rules, and one draw needn't show every extreme that they name: `tile_index`: slot s of an output tile belongs to inner group g = s // 8 and names a left tile of that group, g * 8 to g * 8 + 7; the tiles named by one output tile's slots of one group are distinct. `slot_mask`: in each output tile and inner group the live slots come first and there is at least one; in every output tile some group has all 8 slots live, and the others at most 4.
All inputs are finite; a program needn't handle non-finite values.
Results may differ from a plain program's by a relative error of at most 0.0045.
Values may be sent and summed in bfloat16 or wider, within the bound.
A program may use at most 64 MiB of HBM per device.

v0:
```python
import math
import jax
import jax.numpy as jnp
from jax import lax
from jax.sharding import PartitionSpec as P

NB = 512
HIGH = lax.Precision.HIGHEST


def orthonormal(sketch_rows, factor):
    solved = jax.scipy.linalg.solve_triangular(factor, jnp.swapaxes(sketch_rows, 1, 2), lower=True)
    return jnp.swapaxes(solved, 1, 2)


def gram_of(sketch_rows):
    return jnp.einsum("ona,onb->oab", sketch_rows, sketch_rows, precision=HIGH)


def body(left_u, left_v, right_u, right_v, sketch, tile_index, slot_mask):
    group_u, group_v = (
        lax.all_gather(left_u, "cols", axis=0, tiled=True),
        lax.all_gather(left_v, "cols", axis=0, tiled=True),
    )
    group_tiles = group_u.shape[0]
    local_idx = tile_index - lax.axis_index("inner") * group_tiles
    live_mask = slot_mask.astype(jnp.float32)[..., None, None]
    tile_u = jnp.take(group_u, local_idx, axis=0)
    tile_v = jnp.take(group_v, local_idx, axis=0)
    pairing = jnp.einsum("osna,osnb->osab", tile_v, right_u, preferred_element_type=jnp.float32)
    probes = jnp.einsum("osnb,ont->osbt", right_v, sketch, preferred_element_type=jnp.float32)
    mixing = (live_mask * jnp.einsum("osab,osbt->osat", pairing, probes, precision=HIGH)).astype(
        jnp.bfloat16
    )
    partial_sketch = jnp.einsum(
        "osna,osat->ont", tile_u, mixing, preferred_element_type=jnp.float32
    )
    scale_up = math.sqrt(NB)
    summed = lax.psum(partial_sketch, "inner")
    factor = jnp.linalg.cholesky(gram_of(summed))
    ortho = orthonormal(summed, factor)
    row_count = summed.shape[1] // lax.axis_size("inner")
    row_start = lax.axis_index("inner") * row_count
    basis = lax.dynamic_slice_in_dim(ortho, row_start, row_count, 1) * scale_up
    full_basis = ortho.astype(jnp.bfloat16)
    projected = jnp.einsum("osna,ont->osat", tile_u, full_basis, preferred_element_type=jnp.float32)
    backward = (
        live_mask * jnp.einsum("osab,osat->osbt", pairing, projected, precision=HIGH)
    ).astype(jnp.bfloat16)
    coeff_terms = jnp.einsum(
        "osnb,osbt->ont", right_v, backward, preferred_element_type=jnp.float32
    )
    coeff = lax.psum_scatter(coeff_terms, "inner", scatter_dimension=1, tiled=True)
    return (basis, coeff)


def solution(mesh):
    return jax.shard_map(
        body,
        mesh=mesh,
        in_specs=(
            P(("inner", "cols"), None, None),
            P(("inner", "cols"), None, None),
            P("cols", "inner", None, None),
            P("cols", "inner", None, None),
            P("cols", None, None),
            P("cols", "inner"),
            P("cols", "inner"),
        ),
        out_specs=(P("cols", "inner", None), P("cols", "inner", None)),
        check_vma=False,
    )
```

profile of v0, /device:TPU:0, one launch (start us, length us, event | category | flops | bytes accessed | tf_op | source)
XLA Modules:
  0.0 335.3 jit_solution(5929237776262730713)
XLA Ops:
  7.2 0.0 copy-start
  7.2 0.0 all-gather.5.cloned.1.call-start
  7.2 0.7 all-gather.5.cloned.1.call-update
  7.9 0.0 all-gather.3.cloned.1.call-start
  8.0 0.7 all-gather.3.cloned.1.call-update
  8.7 0.0 all-reduce.4.cloned.1.call-start
  8.7 0.7 compare_and_fusion
  9.4 0.1 reshape.41
  9.5 0.7 convert_element_type.12
  10.2 0.0 copy-done
  10.2 3.8 %fusion.10 = f32[4,8,128,128]{3,2,1,0:T(8,128)S(1)} fusion(bf16[4,8,512,128]{3,2,1,0:T(8,128)(2,1)} %param.12, bf16[4,512,128]{2,1,0:T(8,128)(2,1)S(1)} %copy-done), kind=kOutput, calls=%fused_computation.16 | convolution fusion | flops 536870912 | bytes 6815744 | tf_op jit(solution)/shard_map/osnb,ont->osbt/dot_general | solution.py:31
  14.0 15.0 %all-gather.5.cloned.1.call-done = bf16[8,512,128]{2,1,0:T(8,128)(2,1)} async-done(((bf16[2,512,128]{2,1,0:T(8,128)(2,1)}), bf16[8,512,128]{2,1,0:T(8,128)(2,1)}) %all-gather.5.cloned.1.call-update) | async-done | bytes 1048592 | tf_op jit(solution)/shard_map/all_gather | solution.py:23
  29.0 4.3 %gather_fusion.1 = bf16[32,512,128]{2,1,0:T(8,128)(2,1)} fusion(bf16[8,512,128]{2,1,0:T(8,128)(2,1)} %all-gather.5.cloned.1.call-done, s32[1024]{0:T(1024)S(1)} %pad_clamp_fusion), kind=kCustom, calls=%fused_computation.1.clone | custom fusion | bytes 8388736 | tf_op jit(solution)/shard_map/jit(_take)/gather | solution.py:29
  33.3 6.3 %copy.23 = bf16[4,8,512,128]{2,3,1,0:T(8,128)(2,1)} copy(bf16[4,8,512,128]{3,2,1,0:T(8,128)(2,1)} %bitcast.43) | data formatting | bytes 8388608 | tf_op jit(solution)/shard_map/jit(_take)/gather | solution.py:29
  39.6 7.7 %all-gather.3.cloned.1.call-done = bf16[8,512,128]{2,1,0:T(8,128)(2,1)} async-done(((bf16[2,512,128]{2,1,0:T(8,128)(2,1)}), bf16[8,512,128]{2,1,0:T(8,128)(2,1)}) %all-gather.3.cloned.1.call-update) | async-done | bytes 1048592 | tf_op jit(solution)/shard_map/all_gather | solution.py:22
  47.3 4.3 %gather_fusion = bf16[32,512,128]{2,1,0:T(8,128)(2,1)} fusion(bf16[8,512,128]{2,1,0:T(8,128)(2,1)} %all-gather.3.cloned.1.call-done, s32[1024]{0:T(1024)S(1)} %pad_clamp_fusion), kind=kCustom, calls=%fused_computation.clone | custom fusion | bytes 8388736 | tf_op jit(solution)/shard_map/jit(_take)/gather | solution.py:28
  51.6 6.2 %copy.22 = bf16[4,8,512,128]{2,3,1,0:T(8,128)(2,1)} copy(bf16[4,8,512,128]{3,2,1,0:T(8,128)(2,1)} %bitcast.42) | data formatting | bytes 8388608 | tf_op jit(solution)/shard_map/jit(_take)/gather | solution.py:28
  57.7 4.8 %fusion = f32[4,8,128,128]{3,2,1,0:T(8,128)S(1)} fusion(bf16[4,8,512,128]{3,2,1,0:T(8,128)(2,1)} %param.11, bf16[4,8,512,128]{2,3,1,0:T(8,128)(2,1)} %copy.23, pred[4,8]{1,0:T(4,128)(4,1)S(1)} %get-tuple-element.9), kind=kOutput, calls=%fused_computation.2 | convolution fusion | flops 538968064 | bytes 10485792 | tf_op jit(solution)/shard_map/osna,osnb->osab/dot_general | solution.py:30
  62.5 0.0 copy-start.3
  62.6 1.3 copy-done.3
  63.9 0.0 copy-start.5
  63.9 2.3 multiply_convert_fusion.1
  66.2 0.0 copy-done.5
  66.2 2.8 fusion.8
  69.0 0.0 all-reduce.4.cloned.1.call-update
  69.0 0.2 all-reduce.6.cloned.1.call-start
  69.3 78.1 %all-reduce.4.cloned.1.call-done = f32[4,512,128]{2,1,0:T(8,128)} async-done(((f32[4,512,128]{2,1,0:T(8,128)}), f32[4,512,128]{2,1,0:T(8,128)}) %all-reduce.4.cloned.1.call-update) | async-done | bytes 1048592 | tf_op jit(solution)/shard_map/psum | solution.py:39
  147.4 0.0 copy-start.2
  147.4 3.4 %fusion.19 = f32[4,128,128]{2,1,0:T(8,128)S(1)} fusion(f32[4,512,128]{2,1,0:T(8,128)} %all-reduce.4.cloned.1.call-done), kind=kOutput, calls=%fused_computation.36 | convolution fusion | flops 402653184 | bytes 1310720 | tf_op jit(solution)/shard_map/ona,onb->oab/dot_general | solution.py:17
  150.8 0.1 copy.27
  151.0 46.9 %custom-call.8 = f32[4,128,128]{2,1,0:T(8,128)S(1)} custom-call(f32[4,128,128]{2,1,0:T(8,128)S(1)} %fusion.15), custom_call_target="Cholesky" | custom-call | tf_op jit(solution)/shard_map/jit(cholesky)/cholesky | solution.py:40
  198.0 0.1 compare_reduce_fusion
  198.1 0.1 select_bitcast_fusion
  198.2 39.5 %custom-call.9 = f32[4,1,128,128]{2,3,1,0:T(8,128)S(1)} custom-call(f32[4,1,128,128]{3,2,1,0:T(8,128)S(1)} %select_bitcast_fusion), custom_call_target="InvertDiagBlocksLowerTriangular" | custom-call | tf_op jit(solution)/shard_map/jit(_solve_triangular)/vmap()/triangular_solve | solution.py:12
  237.7 0.0 copy-done.2
  237.7 1.0 fusion.13
  238.8 0.0 copy-start.4
  238.8 3.6 %fusion.3 = f32[4,8,128,128]{3,2,1,0:T(8,128)S(1)} fusion(bf16[4,8,512,128]{2,3,1,0:T(8,128)(2,1)} %copy.22, pred[4,8]{1,0:T(4,128)(4,1)S(1)} %get-tuple-element.9, f32[4,512,128]{2,1,0:T(8,128)S(1)} %fusion.13), kind=kOutput, calls=%fused_computation.6 | convolution fusion | flops 539230208 | bytes 7340064 | tf_op jit(solution)/shard_map/osna,ont->osat/dot_general | solution.py:46
  242.4 0.0 copy-done.4
  242.4 0.0 copy-start.1
  242.5 3.7 %multiply_convert_fusion = bf16[4,8,128,128]{3,2,1,0:T(8,128)(2,1)S(1)} fusion(f32[4,8,128,128]{3,2,1,0:T(8,128)S(1)} %copy-done.4, f32[4,8,128,128]{3,2,1,0:T(8,128)S(1)} %fusion.3, f32[4,8]{1,0:T(4,128)S(1)} %convert_element_type.12), kind=kOutput, calls=%fused_computation.11 | convolution fusion | flops 806354944 | bytes 5243008 | tf_op jit(solution)/shard_map/osab,osat->osbt/dot_general | solution.py:48
  246.2 0.0 copy-done.1
  246.2 0.0 copy-start.6
  246.2 1.5 convolution_bitcast_fusion
  247.7 1.4 copy.31
  249.1 0.0 all-reduce.6.cloned.1.call-update
  249.1 0.0 copy-done.6
  249.2 0.6 dynamic-slice
  250.4 0.7 dynamic-slice_multiply_fusion
  251.1 76.1 %all-reduce.6.cloned.1.call-done = f32[4,512,128]{2,0,1:T(4,128)} async-done(((f32[4,512,128]{2,0,1:T(4,128)}), f32[4,512,128]{2,0,1:T(4,128)}) %all-reduce.6.cloned.1.call-update) | async-done | bytes 1048592
  327.2 0.9 constant_dynamic-slice_fusion
  328.1 0.7 copy.32
  (5 shorter events, 0.1 us)
Async XLA Ops:
  7.2 3.0 copy-start
  7.2 21.8 %all-gather.5.cloned.1.call-start = ((), (), s32[]{:S(2)}) async-start(), calls=%async_computation.1 | async-start | bytes 1310720 | tf_op jit(solution)/shard_map/all_gather | solution.py:23
  7.9 39.4 %all-gather.3.cloned.1.call-start = ((), (), s32[]{:S(2)}) async-start(), calls=%async_computation | async-start | bytes 1310720 | tf_op jit(solution)/shard_map/all_gather | solution.py:22
  8.7 138.7 %all-reduce.4.cloned.1.call-start = ((), (), s32[]{:S(2)}) async-start(), calls=%async_computation.2 | async-start | bytes 2097152 | tf_op jit(solution)/shard_map/psum | solution.py:39
  62.5 1.3 copy-start.3
  63.9 2.3 copy-start.5
  69.0 258.2 %all-reduce.6.cloned.1.call-start = ((), (), s32[]{:S(2)}) async-start(), calls=%async_computation.3 | async-start | bytes 2097152
  147.4 90.3 %copy-start.2 = (f32[4,512,128]{2,1,0:T(8,128)S(1)}, f32[4,512,128]{2,1,0:T(8,128)}, u32[]{:S(2)}) copy-start(f32[4,512,128]{2,1,0:T(8,128)} %all-reduce.4.cloned.1.call-done) | copy-start | bytes 3145732
  238.8 3.7 %copy-start.4 = (f32[4,8,128,128]{3,2,1,0:T(8,128)S(1)}, f32[4,8,128,128]{3,2,1,0:T(8,128)}, u32[]{:S(2)}) copy-start(f32[4,8,128,128]{3,2,1,0:T(8,128)} %copy-done.3) | copy-start | bytes 6291460
  242.4 3.8 %copy-start.1 = (bf16[4,8,512,128]{3,2,1,0:T(8,128)(2,1)S(1)}, bf16[4,8,512,128]{3,2,1,0:T(8,128)(2,1)}, u32[]{:S(2)}) copy-start(bf16[4,8,512,128]{3,2,1,0:T(8,128)(2,1)} %param.12) | copy-start | bytes 12582916
  246.2 2.9 copy-start.6
Sparse Core Ops, SparseCore 0:
  9.5 19.4 all-gather.4
  30.6 16.6 all-gather.2
  69.1 78.2 all-reduce.3
  249.3 77.8 all-reduce.5
where the time goes:
time: 336 us; the launch traced here: 335 us
  waiting for transfers between devices  178 us (53%)
  other arithmetic  88.8 us (26%)
  matrix products  27 us (8%)
  local copies, waits for them, and re-layouts  26.1 us (8%)
  between operations  14.6 us (4%)
    psum x1, waiting for transfers between devices, body(): summed = lax.psum(partial_sketch, 'inner')  78.1 us
    unnamed x5, waiting for transfers between devices  77.5 us
    another operation x4, other arithmetic, body(): factor = jnp.linalg.cholesky(gram_of(summed))  47.1 us
    another operation x3, other arithmetic, orthonormal(): jax.scipy.linalg.solve_triangular(factor, jnp.swapaxes(sketch_rows, 1, 2)...  39.7 us
    all_gather x1, waiting for transfers between devices, body(): lax.all_gather(left_v, 'cols', axis=0, tiled=True)  15 us
    gather x2, local copies, waits for them, and re-layouts, body(): tile_v = jnp.take(group_v, local_idx, axis=0)  10.6 us
    gather x2, local copies, waits for them, and re-layouts, body(): tile_u = jnp.take(group_u, local_idx, axis=0)  10.5 us
    all_gather x1, waiting for transfers between devices, body(): lax.all_gather(left_u, 'cols', axis=0, tiled=True)  7.72 us
  transfers between devices with their start and end apart: 4, of which 4 were waited for; matrix products, arithmetic and copies ran while one was open for 5% of the time, Pallas kernels for 0%

commit v1 on v0

--- a/solution.py
+++ b/solution.py
@@ -36,7 +36,9 @@
         "osna,osat->ont", tile_u, mixing, preferred_element_type=jnp.float32
     )
     scale_up = math.sqrt(NB)
-    summed = lax.psum(partial_sketch, "inner")
+    summed = partial_sketch
+    for hop in (1, 2, 4):
+        summed = summed + lax.ppermute(summed, "inner", [(dev, dev ^ hop) for dev in range(8)])
     factor = jnp.linalg.cholesky(gram_of(summed))
     ortho = orthonormal(summed, factor)
     row_count = summed.shape[1] // lax.axis_size("inner")

time: 336 us -> 352 us (1.048)
  waiting for transfers between devices: 178 us -> 192 us
  starting transfers between devices: 0.34 us -> 5.68 us
    ppermute x0 -> x3, waiting for transfers between devices: none -> 91.2 us  [body(): lax.ppermute(summed, 'inner', [(dev, dev ^ hop) for dev in range(8)])]
    psum x1 -> x0, waiting for transfers between devices: 78.1 us -> none  [body(): summed = lax.psum(partial_sketch, 'inner')]
    ppermute x0 -> x3, starting transfers between devices: none -> 5.57 us  [body(): lax.ppermute(summed, 'inner', [(dev, dev ^ hop) for dev in range(8)])]
    unnamed x5 -> x4, waiting for transfers between devices: 77.5 us -> 77.9 us
  transfers between devices with their start and end apart: 4 -> 6, of which waited for: 4 -> 6; matrix products, arithmetic and copies ran while one was open for 5% -> 5% of each run, Pallas kernels for 0% -> 0%
where the time goes in v1:
time: 352 us; the launch traced here: 351 us
  waiting for transfers between devices  192 us (55%)
  other arithmetic  89.4 us (25%)
  local copies, waits for them, and re-layouts  25.6 us (7%)
  matrix products  24.4 us (7%)
  between operations  14.6 us (4%)
  starting transfers between devices  5.68 us (2%)
    ppermute x3, waiting for transfers between devices, body(): lax.ppermute(summed, 'inner', [(dev, dev ^ hop) for dev in range(8)])  91.2 us
    unnamed x4, waiting for transfers between devices  77.9 us
    another operation x4, other arithmetic, body(): factor = jnp.linalg.cholesky(gram_of(summed))  47.3 us
    another operation x3, other arithmetic, orthonormal(): jax.scipy.linalg.solve_triangular(factor, jnp.swapaxes(sketch_rows, 1, 2)...  39.7 us
    all_gather x1, waiting for transfers between devices, body(): lax.all_gather(left_v, 'cols', axis=0, tiled=True)  15 us
    gather x2, local copies, waits for them, and re-layouts, body(): tile_v = jnp.take(group_v, local_idx, axis=0)  10.7 us
    gather x2, local copies, waits for them, and re-layouts, body(): tile_u = jnp.take(group_u, local_idx, axis=0)  10.5 us
    all_gather x1, waiting for transfers between devices, body(): lax.all_gather(left_u, 'cols', axis=0, tiled=True)  7.61 us
  transfers between devices with their start and end apart: 6, of which 6 were waited for; matrix products, arithmetic and copies ran while one was open for 5% of the time, Pallas kernels for 0%

profile of v1, /device:TPU:0, one launch (start us, length us, event | category | flops | bytes accessed | tf_op | source)
XLA Modules:
  0.0 351.5 jit_solution(3372208796655425218)
XLA Ops:
  7.2 0.0 copy-start
  7.2 0.0 all-gather.5.cloned.1.call-start
  7.2 0.7 all-gather.5.cloned.1.call-update
  7.9 0.0 all-gather.3.cloned.1.call-start
  8.0 0.7 all-gather.3.cloned.1.call-update
  8.7 0.0 all-reduce.3.cloned.1.call-start
  8.7 0.7 compare_and_fusion
  9.4 0.1 reshape.41
  9.5 0.7 convert_element_type.12
  10.2 0.0 copy-done
  10.2 3.8 %fusion.10 = f32[4,8,128,128]{3,2,1,0:T(8,128)S(1)} fusion(bf16[4,8,512,128]{3,2,1,0:T(8,128)(2,1)} %param.12, bf16[4,512,128]{2,1,0:T(8,128)(2,1)S(1)} %copy-done), kind=kOutput, calls=%fused_computation.16 | convolution fusion | flops 536870912 | bytes 6815744 | tf_op jit(solution)/shard_map/osnb,ont->osbt/dot_general | solution.py:31
  14.0 15.0 %all-gather.5.cloned.1.call-done = bf16[8,512,128]{2,1,0:T(8,128)(2,1)} async-done(((bf16[2,512,128]{2,1,0:T(8,128)(2,1)}), bf16[8,512,128]{2,1,0:T(8,128)(2,1)}) %all-gather.5.cloned.1.call-update) | async-done | bytes 1048592 | tf_op jit(solution)/shard_map/all_gather | solution.py:23
  29.0 4.3 %gather_fusion.1 = bf16[32,512,128]{2,1,0:T(8,128)(2,1)} fusion(bf16[8,512,128]{2,1,0:T(8,128)(2,1)} %all-gather.5.cloned.1.call-done, s32[1024]{0:T(1024)S(1)} %pad_clamp_fusion), kind=kCustom, calls=%fused_computation.1.clone | custom fusion | bytes 8388736 | tf_op jit(solution)/shard_map/jit(_take)/gather | solution.py:29
  33.3 6.3 %copy.23 = bf16[4,8,512,128]{2,3,1,0:T(8,128)(2,1)} copy(bf16[4,8,512,128]{3,2,1,0:T(8,128)(2,1)} %bitcast.43) | data formatting | bytes 8388608 | tf_op jit(solution)/shard_map/jit(_take)/gather | solution.py:29
  39.7 7.6 %all-gather.3.cloned.1.call-done = bf16[8,512,128]{2,1,0:T(8,128)(2,1)} async-done(((bf16[2,512,128]{2,1,0:T(8,128)(2,1)}), bf16[8,512,128]{2,1,0:T(8,128)(2,1)}) %all-gather.3.cloned.1.call-update) | async-done | bytes 1048592 | tf_op jit(solution)/shard_map/all_gather | solution.py:22
  47.3 4.3 %gather_fusion = bf16[32,512,128]{2,1,0:T(8,128)(2,1)} fusion(bf16[8,512,128]{2,1,0:T(8,128)(2,1)} %all-gather.3.cloned.1.call-done, s32[1024]{0:T(1024)S(1)} %pad_clamp_fusion), kind=kCustom, calls=%fused_computation.clone | custom fusion | bytes 8388736 | tf_op jit(solution)/shard_map/jit(_take)/gather | solution.py:28
  51.6 6.3 %copy.22 = bf16[4,8,512,128]{2,3,1,0:T(8,128)(2,1)} copy(bf16[4,8,512,128]{3,2,1,0:T(8,128)(2,1)} %bitcast.42) | data formatting | bytes 8388608 | tf_op jit(solution)/shard_map/jit(_take)/gather | solution.py:28
  57.8 4.8 %fusion = f32[4,8,128,128]{3,2,1,0:T(8,128)S(1)} fusion(bf16[4,8,512,128]{3,2,1,0:T(8,128)(2,1)} %param.11, bf16[4,8,512,128]{2,3,1,0:T(8,128)(2,1)} %copy.23, pred[4,8]{1,0:T(4,128)(4,1)S(1)} %get-tuple-element.9), kind=kOutput, calls=%fused_computation.2 | convolution fusion | flops 538968064 | bytes 10485792 | tf_op jit(solution)/shard_map/osna,osnb->osab/dot_general | solution.py:30
  62.6 0.0 copy-start.2
  62.6 0.0 copy-start.4
  62.7 2.3 multiply_convert_fusion.1
  65.0 0.6 copy-done.4
  65.6 1.8 fusion.8
  67.4 0.0 copy-done.2
  67.4 1.5 collective-permute-start
  68.9 23.8 %collective-permute-done = f32[4,512,128]{2,1,0:T(8,128)S(1)} collective-permute-done((f32[4,512,128]{2,1,0:T(8,128)S(1)}, f32[4,512,128]{2,1,0:T(8,128)S(1)}, u32[]{:S(2)}, u32[]{:S(2)}) %collective-permute-start) | collective-permute-done | bytes 1048608 | tf_op jit(solution)/shard_map/ppermute | solution.py:41
  92.8 0.2 add.32
  92.9 1.5 collective-permute-start.1
  94.5 22.9 %collective-permute-done.1 = f32[4,512,128]{2,1,0:T(8,128)S(1)} collective-permute-done((f32[4,512,128]{2,1,0:T(8,128)S(1)}, f32[4,512,128]{2,1,0:T(8,128)S(1)}, u32[]{:S(2)}, u32[]{:S(2)}) %collective-permute-start.1) | collective-permute-done | bytes 1048608 | tf_op jit(solution)/shard_map/ppermute | solution.py:41
  117.4 0.1 add.33
  117.5 2.5 collective-permute-start.2
  120.1 44.5 %collective-permute-done.2 = f32[4,512,128]{2,1,0:T(8,128)S(1)} collective-permute-done((f32[4,512,128]{2,1,0:T(8,128)S(1)}, f32[4,512,128]{2,1,0:T(8,128)S(1)}, u32[]{:S(2)}, u32[]{:S(2)}) %collective-permute-start.2) | collective-permute-done | bytes 1048608 | tf_op jit(solution)/shard_map/ppermute | solution.py:41
  164.5 0.1 add.34
  164.6 1.8 fusion.19
  166.5 0.1 copy.27
  166.7 47.1 %custom-call.8 = f32[4,128,128]{2,1,0:T(8,128)S(1)} custom-call(f32[4,128,128]{2,1,0:T(8,128)S(1)} %fusion.15), custom_call_target="Cholesky" | custom-call | tf_op jit(solution)/shard_map/jit(cholesky)/cholesky | solution.py:42
  213.8 0.1 compare_reduce_fusion
  213.9 0.1 select_bitcast_fusion
  214.0 39.5 %custom-call.9 = f32[4,1,128,128]{2,3,1,0:T(8,128)S(1)} custom-call(f32[4,1,128,128]{3,2,1,0:T(8,128)S(1)} %select_bitcast_fusion), custom_call_target="InvertDiagBlocksLowerTriangular" | custom-call | tf_op jit(solution)/shard_map/jit(_solve_triangular)/vmap()/triangular_solve | solution.py:12
  253.5 1.0 fusion.13
  254.6 0.0 copy-start.3
  254.6 3.6 %fusion.3 = f32[4,8,128,128]{3,2,1,0:T(8,128)S(1)} fusion(bf16[4,8,512,128]{2,3,1,0:T(8,128)(2,1)} %copy.22, pred[4,8]{1,0:T(4,128)(4,1)S(1)} %get-tuple-element.9, f32[4,512,128]{2,1,0:T(8,128)S(1)} %fusion.13), kind=kOutput, calls=%fused_computation.6 | convolution fusion | flops 539230208 | bytes 7340064 | tf_op jit(solution)/shard_map/osna,ont->osat/dot_general | solution.py:48
  258.2 0.0 copy-done.3
  258.3 0.0 copy-start.1
  258.3 3.7 %multiply_convert_fusion = bf16[4,8,128,128]{3,2,1,0:T(8,128)(2,1)S(1)} fusion(f32[4,8,128,128]{3,2,1,0:T(8,128)S(1)} %copy-done.3, f32[4,8,128,128]{3,2,1,0:T(8,128)S(1)} %fusion.3, f32[4,8]{1,0:T(4,128)S(1)} %convert_element_type.12), kind=kOutput, calls=%fused_computation.11 | convolution fusion | flops 806354944 | bytes 5243008 | tf_op jit(solution)/shard_map/osab,osat->osbt/dot_general | solution.py:50
  262.0 0.0 copy-done.1
  262.0 0.0 copy-start.5
  262.0 1.5 convolution_bitcast_fusion
  263.6 1.4 copy.31
  264.9 0.0 all-reduce.3.cloned.1.call-update
  264.9 0.0 copy-done.5
  265.0 0.6 dynamic-slice
  266.2 0.7 dynamic-slice_multiply_fusion
  266.9 76.5 %all-reduce.3.cloned.1.call-done = f32[4,512,128]{2,0,1:T(4,128)} async-done(((f32[4,512,128]{2,0,1:T(4,128)}), f32[4,512,128]{2,0,1:T(4,128)}) %all-reduce.3.cloned.1.call-update) | async-done | bytes 1048592
  343.3 0.9 constant_dynamic-slice_fusion
  344.3 0.7 copy.32
  (5 shorter events, 0.1 us)
Async XLA Ops:
  7.2 3.0 copy-start
  7.2 21.8 %all-gather.5.cloned.1.call-start = ((), (), s32[]{:S(2)}) async-start(), calls=%async_computation.1 | async-start | bytes 1310720 | tf_op jit(solution)/shard_map/all_gather | solution.py:23
  7.9 39.4 %all-gather.3.cloned.1.call-start = ((), (), s32[]{:S(2)}) async-start(), calls=%async_computation | async-start | bytes 1310720 | tf_op jit(solution)/shard_map/all_gather | solution.py:22
  8.7 334.7 %all-reduce.3.cloned.1.call-start = ((), (), s32[]{:S(2)}) async-start(), calls=%async_computation.2 | async-start | bytes 2097152
  62.6 4.8 %copy-start.2 = (f32[4,8,128,128]{3,2,1,0:T(8,128)}, f32[4,8,128,128]{3,2,1,0:T(8,128)S(1)}, u32[]{:S(2)}) copy-start(f32[4,8,128,128]{3,2,1,0:T(8,128)S(1)} %fusion) | copy-start | bytes 6291460
  62.6 2.9 copy-start.4
  67.4 25.4 %collective-permute-start = (f32[4,512,128]{2,1,0:T(8,128)S(1)}, f32[4,512,128]{2,1,0:T(8,128)S(1)}, u32[]{:S(2)}, u32[]{:S(2)}) collective-permute-start(f32[4,512,128]{2,1,0:T(8,128)S(1)} %fusion.8), channel_id=1, source_target_pairs={{0,4},{4,0},{8,12},{12,8},{16,20},{20,16},{24,28},{28,24},{1,5},{5... | collective-permute-start | bytes 3145736 | tf_op jit(solution)/shard_map/ppermute | solution.py:41
  92.9 24.5 %collective-permute-start.1 = (f32[4,512,128]{2,1,0:T(8,128)S(1)}, f32[4,512,128]{2,1,0:T(8,128)S(1)}, u32[]{:S(2)}, u32[]{:S(2)}) collective-permute-start(f32[4,512,128]{2,1,0:T(8,128)S(1)} %add.32), channel_id=1, source_target_pairs={{0,8},{4,12},{8,0},{12,4},{16,24},{20,28},{24,16},{28,20},{1,9},{5... | collective-permute-start | bytes 3145736 | tf_op jit(solution)/shard_map/ppermute | solution.py:41
  117.5 47.0 %collective-permute-start.2 = (f32[4,512,128]{2,1,0:T(8,128)S(1)}, f32[4,512,128]{2,1,0:T(8,128)S(1)}, u32[]{:S(2)}, u32[]{:S(2)}) collective-permute-start(f32[4,512,128]{2,1,0:T(8,128)S(1)} %add.33), channel_id=1, source_target_pairs={{0,16},{4,20},{8,24},{12,28},{16,0},{20,4},{24,8},{28,12},{1,17},{... | collective-permute-start | bytes 3145736 | tf_op jit(solution)/shard_map/ppermute | solution.py:41
  254.6 3.7 %copy-start.3 = (f32[4,8,128,128]{3,2,1,0:T(8,128)S(1)}, f32[4,8,128,128]{3,2,1,0:T(8,128)}, u32[]{:S(2)}) copy-start(f32[4,8,128,128]{3,2,1,0:T(8,128)} %copy-done.2) | copy-start | bytes 6291460
  258.3 3.8 %copy-start.1 = (bf16[4,8,512,128]{3,2,1,0:T(8,128)(2,1)S(1)}, bf16[4,8,512,128]{3,2,1,0:T(8,128)(2,1)}, u32[]{:S(2)}) copy-start(bf16[4,8,512,128]{3,2,1,0:T(8,128)(2,1)} %param.12) | copy-start | bytes 12582916
  262.0 2.9 copy-start.5
Sparse Core Ops, SparseCore 0:
  9.5 19.4 all-gather.4
  30.6 16.6 all-gather.2
  265.1 78.2 all-reduce.2
